TPU v7x, 512 devices: a whole 4x8x8 slice. The times are simulated.
512 devices in a mesh: group: 16 (over y, core), inner: 32 (over x, z).
Axes of the slice: x: 4, y: 8, z: 8, core: 2. Of those that a mesh axis runs over, the one named last changes fastest.
Arguments:
- pair_rows: bfloat16 [8192, 2048], P(('group', 'inner')), may hold values from -6 to 6
- group_ids: int32 [8192, 1], P(('group', 'inner')), may hold values from 0 to 15; in each aligned block of 16 rows (0 to 15, 16 to 31, ...) at most 2 rows name the same one
- local_ids: int32 [8192, 1], P(('group', 'inner')), may hold values from 0 to 1
- route_weight: float32 [8192], P(('group', 'inner')), may hold values from 0.3 to 1
- w_up: bfloat16 [32, 2048, 8192], P('group', None, 'inner'), may hold values from -0.125 to 0.125
- w_down: bfloat16 [32, 8192, 2048], P('group', 'inner'), may hold values from -0.0625 to 0.0625
Outputs:
- mixed: bfloat16 [8192, 2048], P(('group', 'inner'))
Inputs may be any that keep to these rules, and one draw needn't show every extreme that they name: `group_ids`: among the rows of one device no value is named more than 2 times, a bound that some block reaches.
All inputs are finite; a program needn't handle non-finite values.
Results may differ from a plain program's by a relative error of at most 0.02.
Values may be sent and summed in bfloat16 or wider, within the bound.
A program may use at most 64 MiB of HBM per device.

v0:
```python
import jax
import jax.numpy as jnp
from jax import lax
from jax.sharding import PartitionSpec as P


def body(pair_rows, group_ids, local_ids, route_weight, w_up, w_down):
    groups = lax.axis_size("group")
    inner_size = lax.axis_size("inner")
    count_rows = pair_rows.shape[0]
    model_width = pair_rows.shape[1]
    local_count = w_up.shape[0]
    capacity = 2 * count_rows // groups
    group_of = group_ids[:, 0]
    onehot = (group_of[:, None] == jnp.arange(groups, dtype=jnp.int32)[None, :]).astype(jnp.int32)
    rank_in = jnp.sum((jnp.cumsum(onehot, 0) - onehot) * onehot, 1)
    target = group_of * capacity + rank_in
    placing = (jnp.arange(groups * capacity, dtype=jnp.int32)[:, None] == target[None, :]).astype(
        jnp.bfloat16
    )
    outgoing = jnp.dot(placing, pair_rows, preferred_element_type=jnp.float32).astype(jnp.bfloat16)
    outgoing = outgoing.reshape(1, groups, capacity, model_width)
    tag_rows = (local_ids[:, 0] + 1).astype(jnp.bfloat16)
    tags = jnp.dot(placing, tag_rows, preferred_element_type=jnp.float32).astype(jnp.bfloat16)
    tags = tags.reshape(1, groups, capacity)
    arrived, arrived_tags = (
        lax.all_to_all(outgoing, "group", split_axis=1, concat_axis=1, tiled=True),
        lax.all_to_all(tags, "group", split_axis=1, concat_axis=1, tiled=True),
    )
    gathered, gathered_tags = (
        lax.all_gather(arrived, "inner", axis=0, tiled=True),
        lax.all_gather(arrived_tags, "inner", axis=0, tiled=True),
    )
    slots = gathered.reshape(inner_size * groups * capacity, model_width)
    slot_tags = gathered_tags.reshape(inner_size * groups * capacity).astype(jnp.float32)
    expert_index = jnp.arange(local_count, dtype=jnp.float32) + 1.0
    own_rows = groups * capacity
    selector = (slot_tags[:, None] == expert_index[None, :]).astype(jnp.float32)
    up_val = jnp.einsum("rd,edf->ref", slots, w_up, preferred_element_type=jnp.float32)
    hidden = (jax.nn.silu(up_val) * selector[:, :, None]).astype(jnp.bfloat16)
    every_term = jnp.einsum("ref,efd->rd", hidden, w_down, preferred_element_type=jnp.float32)
    totals = lax.psum(every_term.astype(jnp.bfloat16), "inner").astype(jnp.float32)
    summed = lax.dynamic_slice_in_dim(totals, lax.axis_index("inner") * own_rows, own_rows, 0)
    send_back = summed.astype(jnp.bfloat16).reshape(groups, capacity, model_width)
    returned = lax.all_to_all(send_back, "group", split_axis=0, concat_axis=0, tiled=True)
    combined = jnp.dot(
        placing.T,
        returned.reshape(groups * capacity, model_width),
        preferred_element_type=jnp.float32,
    )
    return (combined * route_weight[:, None]).astype(jnp.bfloat16)


def solution(mesh):
    placed = (
        P(("group", "inner"), None),
        P(("group", "inner"), None),
        P(("group", "inner"), None),
        P(("group", "inner")),
        P("group", None, "inner"),
        P("group", "inner", None),
    )
    return jax.shard_map(
        body, mesh=mesh, in_specs=placed, out_specs=P(("group", "inner"), None), check_vma=False
    )
```

profile of v0, /device:TPU:1, one launch (start us, length us, event | category | flops | bytes accessed | tf_op | source)
XLA Modules:
  0.0 338.9 jit_solution(1572055282033931939)
XLA Ops:
  6.5 0.9 fusion.5
  7.5 0.8 select_reduce_fusion
  8.3 0.7 multiply_add_fusion
  9.0 1.0 convolution_convert_fusion
  10.0 0.1 reshape.67
  10.1 18.5 %all_to_all.15 = bf16[1,16,2,2048]{3,2,0,1:T(2,128)(2,1)S(1)} all-to-all(bf16[1,16,2,2048]{3,2,0,1:T(2,128)(2,1)S(1)} %bitcast.15), channel_id=1, replica_groups=mesh['group'=16,'inner'=32] {'group'}, dimensions={1} | all-to-all | bytes 262144 | tf_op jit(solution)/shard_map/all_to_all | solution.py:27
  28.6 0.7 copy.14
  29.3 0.8 fusion.1
  30.1 0.7 reshape.78
  30.8 3.4 all-to-all-start.1
  34.2 6.5 %all-to-all-done.1 = bf16[1,16,2]{2,0,1:T(2,128)(2,1)S(1)} async-done(((bf16[1,16,2]{2,0,1:T(2,128)(2,1)}), bf16[1,16,2]{2,0,1:T(2,128)(2,1)S(1)}, u32[]{:S(2)}, u32[]{:S(2)}) %all-to-all-start.1) | async-done | bytes 96 | tf_op jit(solution)/shard_map/all_to_all | solution.py:28
  40.7 0.1 copy.17
  40.8 37.2 %all_gather.7 = bf16[32,16,2]{1,2,0:T(2,128)(2,1)S(1)} all-gather(bf16[1,16,2]{1,2,0:T(2,128)(2,1)S(1)} %copy.17), channel_id=1, replica_groups=mesh['group'=16,'inner'=32] {'inner'}, dimensions={0}, use_global_device_ids=true | all-gather | bytes 2112 | tf_op jit(solution)/shard_map/all_gather | solution.py:32
  78.1 0.2 copy.19
  78.3 0.2 reshape.72
  78.5 34.5 %all-gather.2.cloned.1.call-done = bf16[32,16,2,2048]{3,1,2,0:T(8,128)(2,1)} async-done(((bf16[1,16,2,2048]{3,1,2,0:T(8,128)(2,1)}), bf16[32,16,2,2048]{3,1,2,0:T(8,128)(2,1)}) %all-gather.2.cloned.1.call-update) | async-done | bytes 4194320 | tf_op jit(solution)/shard_map/all_gather | solution.py:31
  113.1 8.5 %copy.15 = bf16[32,16,2,2048]{3,2,1,0:T(2,128)(2,1)} copy(bf16[32,16,2,2048]{3,1,2,0:T(8,128)(2,1)} %all-gather.2.cloned.1.call-done) | data formatting | bytes 8388608 | tf_op jit(solution)/shard_map/all_gather | solution.py:31
  121.6 7.2 %reshape.73 = bf16[1024,2048,1]{1,0,2:T(8,128)(2,1)} reshape(bf16[32,16,2,2048]{3,2,1,0:T(2,128)(2,1)} %copy.15) | data formatting | bytes 8388608 | tf_op jit(solution)/shard_map/reshape | solution.py:34
  128.8 9.5 %bitcast_convert_fusion = bf16[1024,2048]{1,0:T(8,128)(2,1)} fusion(bf16[2,256,2048]{2,1,0:T(8,128)(2,1)S(1)} %copy-done, bf16[1024,2048,1]{1,0,2:T(8,128)(2,1)} %reshape.73, bf16[2,2048,256]{2,1,0:T(8,128)(2,1)} %param.10, f32[1024,2]{0,1:T(2,128)S(1)} %compare_convert_fusion), kind=kOutput, calls=%fused_computation | convolution fusion | flops 4300210176 | bytes 12591104 | tf_op jit(solution)/shard_map/ref,efd->rd/dot_general | solution.py:41
  138.4 172.9 %all-reduce.2.cloned.1.call-done = bf16[1024,2048]{1,0:T(8,128)(2,1)} async-done(((bf16[1024,2048]{1,0:T(8,128)(2,1)}), bf16[1024,2048]{1,0:T(8,128)(2,1)}) %all-reduce.2.cloned.1.call-update) | async-done | bytes 4194320 | tf_op jit(solution)/shard_map/psum | solution.py:42
  311.2 0.9 convert_convert_fusion
  312.1 0.1 reshape.70
  312.2 19.0 %all_to_all.16 = bf16[16,2,2048]{2,1,0:T(2,128)(2,1)S(1)} all-to-all(bf16[16,2,2048]{2,1,0:T(2,128)(2,1)S(1)} %reshape.70), channel_id=1, replica_groups=mesh['group'=16,'inner'=32] {'group'}, dimensions={0} | all-to-all | bytes 262144 | tf_op jit(solution)/shard_map/all_to_all | solution.py:45
  331.3 0.8 fusion
  (13 shorter events, 0.3 us)
Async XLA Ops:
  6.5 122.3 %copy-start = (bf16[2,256,2048]{2,1,0:T(8,128)(2,1)S(1)}, bf16[2,256,2048]{2,1,0:T(8,128)(2,1)}, u32[]{:S(2)}) copy-start(bf16[2,256,2048]{2,1,0:T(8,128)(2,1)} %param.11) | copy-start | bytes 6291460
  6.5 106.6 %all-gather.2.cloned.1.call-start = ((), (), s32[]{:S(2)}) async-start(), calls=%async_computation.3 | async-start | bytes 4325376 | tf_op jit(solution)/shard_map/all_gather | solution.py:31
  30.8 9.9 %all-to-all-start.1 = ((bf16[1,16,2]{2,0,1:T(2,128)(2,1)}), bf16[1,16,2]{2,0,1:T(2,128)(2,1)S(1)}, u32[]{:S(2)}, u32[]{:S(2)}) async-start(bf16[1,16,2]{2,0,1:T(2,128)(2,1)} %reshape.78), calls=%async_computation.1 | async-start | bytes 16384 | tf_op jit(solution)/shard_map/all_to_all | solution.py:28
  34.1 277.1 %all-reduce.2.cloned.1.call-start = ((), (), s32[]{:S(2)}) async-start(), calls=%async_computation.4 | async-start | bytes 8388608 | tf_op jit(solution)/shard_map/psum | solution.py:42
  138.3 192.9 %copy-start.1 = (f32[16]{0:T(128)S(1)}, f32[16]{0:T(128)}, u32[]{:S(2)}) copy-start(f32[16]{0:T(128)} %param.9) | copy-start | bytes 196
Sparse Core Ops, SparseCore 0:
  29.4 83.6 all-gather.1
  138.5 172.6 all-reduce.1
where the time goes:
time: 339 us
  waiting for transfers between devices  214 us (63%)
  blocking collectives  74.7 us (22%)
  local copies, waits for them, and re-layouts  17.9 us (5%)
  between operations  13.5 us (4%)
  matrix products  12.1 us (4%)
  starting transfers between devices  3.41 us (1%)
  other arithmetic  3.41 us (1%)
    psum x1, waiting for transfers between devices, body(): lax.psum(every_term.astype(jnp.bfloat16), 'inner').astype(jnp.float32)  173 us
    all_gather x1, blocking collectives, body(): lax.all_gather(arrived_tags, 'inner', axis=0, tiled=True)  37.2 us
    all_gather x1, waiting for transfers between devices, body(): lax.all_gather(arrived, 'inner', axis=0, tiled=True)  34.5 us
    all_to_all x1, blocking collectives, body(): lax.all_to_all(send_back, 'group', split_axis=0, concat_axis=0, tiled=True)  19 us
    all_to_all x1, blocking collectives, body(): lax.all_to_all(outgoing, 'group', split_axis=1, concat_axis=1, tiled=True)  18.5 us
    dot_general x1, matrix products, body(): jnp.einsum('ref,efd->rd', hidden, w_down, preferred_element_type=jnp.floa...  9.51 us
    all_gather x1, local copies, waits for them, and re-layouts, body(): lax.all_gather(arrived, 'inner', axis=0, tiled=True)  8.52 us
    reshape x1, local copies, waits for them, and re-layouts, body(): slots = gathered.reshape(inner_size * groups * capacity, model_width)  7.19 us
  transfers between devices with their start and end apart: 3, of which 3 were waited for; matrix products, arithmetic and copies ran while one was open for 1% of the time, Pallas kernels for 0%

commit v1 on v0

--- a/solution.py
+++ b/solution.py
@@ -1,7 +1,33 @@
+import functools
 import jax
 import jax.numpy as jnp
 from jax import lax
 from jax.sharding import PartitionSpec as P
+
+
+def place_streams(sample, axis_name):
+    long_array = lax.axis_index(axis_name)
+    front = lax.axis_size(axis_name)
+    part_now, r1 = (front, long_array)
+    even = list(sample.shape)
+    reply = sample.shape[1] // part_now
+    even[1] = reply
+    carry_out = even[1]
+    even[1] = carry_out * part_now
+    pp = 0
+    met_up = jnp.zeros(even, sample.dtype)
+    while pp < part_now:
+        f_next = lax.dynamic_slice_in_dim(sample, (r1 ^ pp) * reply, reply, axis=1)
+        if pp:
+            f_next = lax.ppermute(
+                f_next, axis_name, [(src_i, src_i ^ pp) for src_i in range(part_now)]
+            )
+        met_up = lax.dynamic_update_slice_in_dim(met_up, f_next, (r1 ^ pp) * carry_out, axis=1)
+        pp = pp + 1
+    return met_up
+
+
+wires_try_all = functools.partial(place_streams, axis_name="group")
 
 
 def body(pair_rows, group_ids, local_ids, route_weight, w_up, w_down):
@@ -24,7 +50,7 @@
     tags = jnp.dot(placing, tag_rows, preferred_element_type=jnp.float32).astype(jnp.bfloat16)
     tags = tags.reshape(1, groups, capacity)
     arrived, arrived_tags = (
-        lax.all_to_all(outgoing, "group", split_axis=1, concat_axis=1, tiled=True),
+        wires_try_all(outgoing),
         lax.all_to_all(tags, "group", split_axis=1, concat_axis=1, tiled=True),
     )
     gathered, gathered_tags = (

time: 339 us -> 387 us (1.14)
  starting transfers between devices: 3.41 us -> 65.1 us
  blocking collectives: 74.7 us -> 56 us
    ppermute x0 -> x15, starting transfers between devices: none -> 60.6 us  [place_streams(): lax.ppermute(f_next, axis_name, [(src_i, src_i ^ pp) for src_i in range(p...]
    all_to_all x1 -> x0, blocking collectives: 18.5 us -> none  [body(): lax.all_to_all(outgoing, 'group', split_axis=1, concat_axis=1, tiled=True)]
  transfers between devices with their start and end apart: 3 -> 18, of which waited for: 3 -> 3; matrix products, arithmetic and copies ran while one was open for 1% -> 1% of each run, Pallas kernels for 0% -> 0%
where the time goes in v1:
time: 387 us; the launch traced here: 386 us
  waiting for transfers between devices  215 us (56%)
  starting transfers between devices  65.1 us (17%)
  blocking collectives  56 us (14%)
  local copies, waits for them, and re-layouts  20.6 us (5%)
  between operations  14.1 us (4%)
  matrix products  11.5 us (3%)
    psum x1, waiting for transfers between devices, body(): lax.psum(every_term.astype(jnp.bfloat16), 'inner').astype(jnp.float32)  173 us
    ppermute x15, starting transfers between devices, place_streams(): lax.ppermute(f_next, axis_name, [(src_i, src_i ^ pp) for src_i in range(p...  60.6 us
    all_gather x1, blocking collectives, body(): lax.all_gather(arrived_tags, 'inner', axis=0, tiled=True)  37.1 us
    all_gather x1, waiting for transfers between devices, body(): lax.all_gather(arrived, 'inner', axis=0, tiled=True)  35.3 us
    all_to_all x1, blocking collectives, body(): lax.all_to_all(send_back, 'group', split_axis=0, concat_axis=0, tiled=True)  19 us
    dot_general x1, matrix products, body(): jnp.einsum('ref,efd->rd', hidden, w_down, preferred_element_type=jnp.floa...  9.53 us
    all_gather x1, local copies, waits for them, and re-layouts, body(): lax.all_gather(arrived, 'inner', axis=0, tiled=True)  8.54 us
  transfers between devices with their start and end apart: 18, of which 3 were waited for; matrix products, arithmetic and copies ran while one was open for 1% of the time, Pallas kernels for 0%

profile of v1, /device:TPU:1, one launch (start us, length us, event | category | flops | bytes accessed | tf_op | source)
XLA Modules:
  0.0 385.9 jit_solution(6148536147516319707)
XLA Ops:
  10.4 8.8 %collective-permute-start = (bf16[1,1,2,2048]{3,1,2,0:T(2,128)(2,1)S(1)}, bf16[1,1,2,2048]{3,1,2,0:T(2,128)(2,1)S(1)}, u32[]{:S(2)}, u32[]{:S(2)}) collective-permute-start(bf16[1,1,2,2048]{3,1,2,0:T(2,128)(2,1)S(1)} %copy.49), channel_id=1, source_target_pairs={{0,32},{32,0},{64,96},{96,64},{128,160},{160,128},{192,224},{224,1... | collective-permute-start | bytes 24584 | tf_op jit(solution)/shard_map/ppermute | solution.py:22
  19.2 1.9 collective-permute-start.1
  21.1 3.5 collective-permute-start.2
  24.7 1.9 collective-permute-start.3
  26.6 4.6 %collective-permute-start.4 = (bf16[1,1,2,2048]{3,1,2,0:T(2,128)(2,1)S(1)}, bf16[1,1,2,2048]{3,1,2,0:T(2,128)(2,1)S(1)}, u32[]{:S(2)}, u32[]{:S(2)}) collective-permute-start(bf16[1,1,2,2048]{3,1,2,0:T(2,128)(2,1)S(1)} %copy.53), channel_id=1, source_target_pairs={{0,160},{32,128},{64,224},{96,192},{128,32},{160,0},{192,96},{224,... | collective-permute-start | bytes 24584 | tf_op jit(solution)/shard_map/ppermute | solution.py:22
  31.4 1.9 collective-permute-start.5
  33.4 5.3 %collective-permute-start.6 = (bf16[1,1,2,2048]{3,1,2,0:T(2,128)(2,1)S(1)}, bf16[1,1,2,2048]{3,1,2,0:T(2,128)(2,1)S(1)}, u32[]{:S(2)}, u32[]{:S(2)}) collective-permute-start(bf16[1,1,2,2048]{3,1,2,0:T(2,128)(2,1)S(1)} %copy.55), channel_id=1, source_target_pairs={{0,224},{32,192},{64,160},{96,128},{128,96},{160,64},{192,32},{224... | collective-permute-start | bytes 24584 | tf_op jit(solution)/shard_map/ppermute | solution.py:22
  38.7 2.1 collective-permute-start.7
  40.8 7.5 %collective-permute-start.8 = (bf16[1,1,2,2048]{3,1,2,0:T(2,128)(2,1)S(1)}, bf16[1,1,2,2048]{3,1,2,0:T(2,128)(2,1)S(1)}, u32[]{:S(2)}, u32[]{:S(2)}) collective-permute-start(bf16[1,1,2,2048]{3,1,2,0:T(2,128)(2,1)S(1)} %copy.57), channel_id=1, source_target_pairs={{0,288},{32,256},{64,352},{96,320},{128,416},{160,384},{192,480},{... | collective-permute-start | bytes 24584 | tf_op jit(solution)/shard_map/ppermute | solution.py:22
  48.3 1.9 collective-permute-start.9
  50.4 6.5 %collective-permute-start.10 = (bf16[1,1,2,2048]{3,1,2,0:T(2,128)(2,1)S(1)}, bf16[1,1,2,2048]{3,1,2,0:T(2,128)(2,1)S(1)}, u32[]{:S(2)}, u32[]{:S(2)}) collective-permute-start(bf16[1,1,2,2048]{3,1,2,0:T(2,128)(2,1)S(1)} %copy.59), channel_id=1, source_target_pairs={{0,352},{32,320},{64,288},{96,256},{128,480},{160,448},{192,416},{... | collective-permute-start | bytes 24584 | tf_op jit(solution)/shard_map/ppermute | solution.py:22
  56.9 1.9 collective-permute-start.11
  58.9 5.9 %collective-permute-start.12 = (bf16[1,1,2,2048]{3,1,2,0:T(2,128)(2,1)S(1)}, bf16[1,1,2,2048]{3,1,2,0:T(2,128)(2,1)S(1)}, u32[]{:S(2)}, u32[]{:S(2)}) collective-permute-start(bf16[1,1,2,2048]{3,1,2,0:T(2,128)(2,1)S(1)} %copy.61), channel_id=1, source_target_pairs={{0,416},{32,384},{64,480},{96,448},{128,288},{160,256},{192,352},{... | collective-permute-start | bytes 24584 | tf_op jit(solution)/shard_map/ppermute | solution.py:22
  64.7 1.9 collective-permute-start.13
  66.7 4.8 %collective-permute-start.14 = (bf16[1,1,2,2048]{3,1,2,0:T(2,128)(2,1)S(1)}, bf16[1,1,2,2048]{3,1,2,0:T(2,128)(2,1)S(1)}, u32[]{:S(2)}, u32[]{:S(2)}) collective-permute-start(bf16[1,1,2,2048]{3,1,2,0:T(2,128)(2,1)S(1)} %copy.63), channel_id=1, source_target_pairs={{0,480},{32,448},{64,416},{96,384},{128,352},{160,320},{192,288},{... | collective-permute-start | bytes 24584 | tf_op jit(solution)/shard_map/ppermute | solution.py:22
  75.5 4.5 %all-to-all-start = ((bf16[1,16,2]{2,0,1:T(2,128)(2,1)}), bf16[1,16,2]{2,0,1:T(2,128)(2,1)S(1)}, u32[]{:S(2)}, u32[]{:S(2)}) async-start(bf16[1,16,2]{2,0,1:T(2,128)(2,1)} %reshape.78), calls=%async_computation | async-start | bytes 16384 | tf_op jit(solution)/shard_map/all_to_all | solution.py:54
  80.0 6.9 %all-to-all-done = bf16[1,16,2]{2,0,1:T(2,128)(2,1)S(1)} async-done(((bf16[1,16,2]{2,0,1:T(2,128)(2,1)}), bf16[1,16,2]{2,0,1:T(2,128)(2,1)S(1)}, u32[]{:S(2)}, u32[]{:S(2)}) %all-to-all-start) | async-done | bytes 96 | tf_op jit(solution)/shard_map/all_to_all | solution.py:54
  87.0 37.1 %all_gather.7 = bf16[32,16,2]{1,2,0:T(2,128)(2,1)S(1)} all-gather(bf16[1,16,2]{1,2,0:T(2,128)(2,1)S(1)} %copy.45), channel_id=1, replica_groups=mesh['group'=16,'inner'=32] {'inner'}, dimensions={0}, use_global_device_ids=true | all-gather | bytes 2112 | tf_op jit(solution)/shard_map/all_gather | solution.py:58
  124.6 35.3 %all-gather.2.cloned.1.call-done = bf16[32,16,2,2048]{3,1,2,0:T(8,128)(2,1)} async-done(((bf16[1,16,2,2048]{3,1,2,0:T(8,128)(2,1)}), bf16[32,16,2,2048]{3,1,2,0:T(8,128)(2,1)}) %all-gather.2.cloned.1.call-update) | async-done | bytes 4194320 | tf_op jit(solution)/shard_map/all_gather | solution.py:57
  159.9 8.5 %copy.43 = bf16[32,16,2,2048]{3,2,1,0:T(2,128)(2,1)} copy(bf16[32,16,2,2048]{3,1,2,0:T(8,128)(2,1)} %all-gather.2.cloned.1.call-done) | data formatting | bytes 8388608 | tf_op jit(solution)/shard_map/all_gather | solution.py:57
  168.5 7.2 %reshape.73 = bf16[1024,2048,1]{1,0,2:T(8,128)(2,1)} reshape(bf16[32,16,2,2048]{3,2,1,0:T(2,128)(2,1)} %copy.43) | data formatting | bytes 8388608 | tf_op jit(solution)/shard_map/reshape | solution.py:60
  175.7 9.5 %bitcast_convert_fusion = bf16[1024,2048]{1,0:T(8,128)(2,1)} fusion(bf16[2,256,2048]{2,1,0:T(8,128)(2,1)S(1)} %copy-done, bf16[1024,2048,1]{1,0,2:T(8,128)(2,1)} %reshape.73, bf16[2,2048,256]{2,1,0:T(8,128)(2,1)} %param.10, f32[1024,2]{0,1:T(2,128)S(1)} %compare_convert_fusion), kind=kOutput, calls=%fused_computation | convolution fusion | flops 4300210176 | bytes 12591104 | tf_op jit(solution)/shard_map/ref,efd->rd/dot_general | solution.py:67
  185.2 173.0 %all-reduce.2.cloned.1.call-done = bf16[1024,2048]{1,0:T(8,128)(2,1)} async-done(((bf16[1024,2048]{1,0:T(8,128)(2,1)}), bf16[1024,2048]{1,0:T(8,128)(2,1)}) %all-reduce.2.cloned.1.call-update) | async-done | bytes 4194320 | tf_op jit(solution)/shard_map/psum | solution.py:68
  359.2 19.0 %all_to_all.10 = bf16[16,2,2048]{2,1,0:T(2,128)(2,1)S(1)} all-to-all(bf16[16,2,2048]{2,1,0:T(2,128)(2,1)S(1)} %reshape.70), channel_id=1, replica_groups=mesh['group'=16,'inner'=32] {'group'}, dimensions={0} | all-to-all | bytes 262144 | tf_op jit(solution)/shard_map/all_to_all | solution.py:71
  (79 shorter events, 10.4 us)
Async XLA Ops:
  6.5 169.1 %copy-start = (bf16[2,256,2048]{2,1,0:T(8,128)(2,1)S(1)}, bf16[2,256,2048]{2,1,0:T(8,128)(2,1)}, u32[]{:S(2)}) copy-start(bf16[2,256,2048]{2,1,0:T(8,128)(2,1)} %param.11) | copy-start | bytes 6291460
  6.5 68.1 %copy-start.3 = (s32[16,1]{0,1:T(1,128)S(1)}, s32[16,1]{0,1:T(1,128)}, u32[]{:S(2)}) copy-start(s32[16,1]{0,1:T(1,128)} %param.8) | copy-start | bytes 196
  6.5 153.4 %all-gather.2.cloned.1.call-start = ((), (), s32[]{:S(2)}) async-start(), calls=%async_computation.2 | async-start | bytes 4325376 | tf_op jit(solution)/shard_map/all_gather | solution.py:57
  10.4 21.1 %collective-permute-start = (bf16[1,1,2,2048]{3,1,2,0:T(2,128)(2,1)S(1)}, bf16[1,1,2,2048]{3,1,2,0:T(2,128)(2,1)S(1)}, u32[]{:S(2)}, u32[]{:S(2)}) collective-permute-start(bf16[1,1,2,2048]{3,1,2,0:T(2,128)(2,1)S(1)} %copy.49), channel_id=1, source_target_pairs={{0,32},{32,0},{64,96},{96,64},{128,160},{160,128},{192,224},{224,1... | collective-permute-start | bytes 24584 | tf_op jit(solution)/shard_map/ppermute | solution.py:22
  19.2 14.2 %collective-permute-start.1 = (bf16[1,1,2,2048]{3,1,2,0:T(2,128)(2,1)S(1)}, bf16[1,1,2,2048]{3,1,2,0:T(2,128)(2,1)S(1)}, u32[]{:S(2)}, u32[]{:S(2)}) collective-permute-start(bf16[1,1,2,2048]{3,1,2,0:T(2,128)(2,1)S(1)} %copy.50), channel_id=1, source_target_pairs={{0,64},{32,96},{64,0},{96,32},{128,192},{160,224},{192,128},{224,1... | collective-permute-start | bytes 24584 | tf_op jit(solution)/shard_map/ppermute | solution.py:22
  21.1 17.6 %collective-permute-start.2 = (bf16[1,1,2,2048]{3,1,2,0:T(2,128)(2,1)S(1)}, bf16[1,1,2,2048]{3,1,2,0:T(2,128)(2,1)S(1)}, u32[]{:S(2)}, u32[]{:S(2)}) collective-permute-start(bf16[1,1,2,2048]{3,1,2,0:T(2,128)(2,1)S(1)} %copy.51), channel_id=1, source_target_pairs={{0,96},{32,64},{64,32},{96,0},{128,224},{160,192},{192,160},{224,1... | collective-permute-start | bytes 24584 | tf_op jit(solution)/shard_map/ppermute | solution.py:22
  24.7 16.1 %collective-permute-start.3 = (bf16[1,1,2,2048]{3,1,2,0:T(2,128)(2,1)S(1)}, bf16[1,1,2,2048]{3,1,2,0:T(2,128)(2,1)S(1)}, u32[]{:S(2)}, u32[]{:S(2)}) collective-permute-start(bf16[1,1,2,2048]{3,1,2,0:T(2,128)(2,1)S(1)} %copy.52), channel_id=1, source_target_pairs={{0,128},{32,160},{64,192},{96,224},{128,0},{160,32},{192,64},{224,... | collective-permute-start | bytes 24584 | tf_op jit(solution)/shard_map/ppermute | solution.py:22
  26.6 21.7 %collective-permute-start.4 = (bf16[1,1,2,2048]{3,1,2,0:T(2,128)(2,1)S(1)}, bf16[1,1,2,2048]{3,1,2,0:T(2,128)(2,1)S(1)}, u32[]{:S(2)}, u32[]{:S(2)}) collective-permute-start(bf16[1,1,2,2048]{3,1,2,0:T(2,128)(2,1)S(1)} %copy.53), channel_id=1, source_target_pairs={{0,160},{32,128},{64,224},{96,192},{128,32},{160,0},{192,96},{224,... | collective-permute-start | bytes 24584 | tf_op jit(solution)/shard_map/ppermute | solution.py:22
  31.4 18.9 %collective-permute-start.5 = (bf16[1,1,2,2048]{3,1,2,0:T(2,128)(2,1)S(1)}, bf16[1,1,2,2048]{3,1,2,0:T(2,128)(2,1)S(1)}, u32[]{:S(2)}, u32[]{:S(2)}) collective-permute-start(bf16[1,1,2,2048]{3,1,2,0:T(2,128)(2,1)S(1)} %copy.54), channel_id=1, source_target_pairs={{0,192},{32,224},{64,128},{96,160},{128,64},{160,96},{192,0},{224,... | collective-permute-start | bytes 24584 | tf_op jit(solution)/shard_map/ppermute | solution.py:22
  33.4 23.6 %collective-permute-start.6 = (bf16[1,1,2,2048]{3,1,2,0:T(2,128)(2,1)S(1)}, bf16[1,1,2,2048]{3,1,2,0:T(2,128)(2,1)S(1)}, u32[]{:S(2)}, u32[]{:S(2)}) collective-permute-start(bf16[1,1,2,2048]{3,1,2,0:T(2,128)(2,1)S(1)} %copy.55), channel_id=1, source_target_pairs={{0,224},{32,192},{64,160},{96,128},{128,96},{160,64},{192,32},{224... | collective-permute-start | bytes 24584 | tf_op jit(solution)/shard_map/ppermute | solution.py:22
  38.7 20.2 %collective-permute-start.7 = (bf16[1,1,2,2048]{3,1,2,0:T(2,128)(2,1)S(1)}, bf16[1,1,2,2048]{3,1,2,0:T(2,128)(2,1)S(1)}, u32[]{:S(2)}, u32[]{:S(2)}) collective-permute-start(bf16[1,1,2,2048]{3,1,2,0:T(2,128)(2,1)S(1)} %copy.56), channel_id=1, source_target_pairs={{0,256},{32,288},{64,320},{96,352},{128,384},{160,416},{192,448},{... | collective-permute-start | bytes 24584 | tf_op jit(solution)/shard_map/ppermute | solution.py:22
  40.8 23.9 %collective-permute-start.8 = (bf16[1,1,2,2048]{3,1,2,0:T(2,128)(2,1)S(1)}, bf16[1,1,2,2048]{3,1,2,0:T(2,128)(2,1)S(1)}, u32[]{:S(2)}, u32[]{:S(2)}) collective-permute-start(bf16[1,1,2,2048]{3,1,2,0:T(2,128)(2,1)S(1)} %copy.57), channel_id=1, source_target_pairs={{0,288},{32,256},{64,352},{96,320},{128,416},{160,384},{192,480},{... | collective-permute-start | bytes 24584 | tf_op jit(solution)/shard_map/ppermute | solution.py:22
  48.3 18.4 %collective-permute-start.9 = (bf16[1,1,2,2048]{3,1,2,0:T(2,128)(2,1)S(1)}, bf16[1,1,2,2048]{3,1,2,0:T(2,128)(2,1)S(1)}, u32[]{:S(2)}, u32[]{:S(2)}) collective-permute-start(bf16[1,1,2,2048]{3,1,2,0:T(2,128)(2,1)S(1)} %copy.58), channel_id=1, source_target_pairs={{0,320},{32,352},{64,256},{96,288},{128,448},{160,480},{192,384},{... | collective-permute-start | bytes 24584 | tf_op jit(solution)/shard_map/ppermute | solution.py:22
  50.4 22.8 %collective-permute-start.10 = (bf16[1,1,2,2048]{3,1,2,0:T(2,128)(2,1)S(1)}, bf16[1,1,2,2048]{3,1,2,0:T(2,128)(2,1)S(1)}, u32[]{:S(2)}, u32[]{:S(2)}) collective-permute-start(bf16[1,1,2,2048]{3,1,2,0:T(2,128)(2,1)S(1)} %copy.59), channel_id=1, source_target_pairs={{0,352},{32,320},{64,288},{96,256},{128,480},{160,448},{192,416},{... | collective-permute-start | bytes 24584 | tf_op jit(solution)/shard_map/ppermute | solution.py:22
  56.9 16.4 %collective-permute-start.11 = (bf16[1,1,2,2048]{3,1,2,0:T(2,128)(2,1)S(1)}, bf16[1,1,2,2048]{3,1,2,0:T(2,128)(2,1)S(1)}, u32[]{:S(2)}, u32[]{:S(2)}) collective-permute-start(bf16[1,1,2,2048]{3,1,2,0:T(2,128)(2,1)S(1)} %copy.60), channel_id=1, source_target_pairs={{0,384},{32,416},{64,448},{96,480},{128,256},{160,288},{192,320},{... | collective-permute-start | bytes 24584 | tf_op jit(solution)/shard_map/ppermute | solution.py:22
  58.9 14.6 %collective-permute-start.12 = (bf16[1,1,2,2048]{3,1,2,0:T(2,128)(2,1)S(1)}, bf16[1,1,2,2048]{3,1,2,0:T(2,128)(2,1)S(1)}, u32[]{:S(2)}, u32[]{:S(2)}) collective-permute-start(bf16[1,1,2,2048]{3,1,2,0:T(2,128)(2,1)S(1)} %copy.61), channel_id=1, source_target_pairs={{0,416},{32,384},{64,480},{96,448},{128,288},{160,256},{192,352},{... | collective-permute-start | bytes 24584 | tf_op jit(solution)/shard_map/ppermute | solution.py:22
  64.7 8.9 %collective-permute-start.13 = (bf16[1,1,2,2048]{3,1,2,0:T(2,128)(2,1)S(1)}, bf16[1,1,2,2048]{3,1,2,0:T(2,128)(2,1)S(1)}, u32[]{:S(2)}, u32[]{:S(2)}) collective-permute-start(bf16[1,1,2,2048]{3,1,2,0:T(2,128)(2,1)S(1)} %copy.62), channel_id=1, source_target_pairs={{0,448},{32,480},{64,384},{96,416},{128,320},{160,352},{192,256},{... | collective-permute-start | bytes 24584 | tf_op jit(solution)/shard_map/ppermute | solution.py:22
  66.7 7.1 %collective-permute-start.14 = (bf16[1,1,2,2048]{3,1,2,0:T(2,128)(2,1)S(1)}, bf16[1,1,2,2048]{3,1,2,0:T(2,128)(2,1)S(1)}, u32[]{:S(2)}, u32[]{:S(2)}) collective-permute-start(bf16[1,1,2,2048]{3,1,2,0:T(2,128)(2,1)S(1)} %copy.63), channel_id=1, source_target_pairs={{0,480},{32,448},{64,416},{96,384},{128,352},{160,320},{192,288},{... | collective-permute-start | bytes 24584 | tf_op jit(solution)/shard_map/ppermute | solution.py:22
  74.0 0.7 copy-start.1
  75.5 11.4 %all-to-all-start = ((bf16[1,16,2]{2,0,1:T(2,128)(2,1)}), bf16[1,16,2]{2,0,1:T(2,128)(2,1)S(1)}, u32[]{:S(2)}, u32[]{:S(2)}) async-start(bf16[1,16,2]{2,0,1:T(2,128)(2,1)} %reshape.78), calls=%async_computation | async-start | bytes 16384 | tf_op jit(solution)/shard_map/all_to_all | solution.py:54
  80.0 278.2 %all-reduce.2.cloned.1.call-start = ((), (), s32[]{:S(2)}) async-start(), calls=%async_computation.3 | async-start | bytes 8388608 | tf_op jit(solution)/shard_map/psum | solution.py:68
  185.2 193.0 %copy-start.2 = (f32[16]{0:T(128)S(1)}, f32[16]{0:T(128)}, u32[]{:S(2)}) copy-start(f32[16]{0:T(128)} %param.9) | copy-start | bytes 196
Sparse Core Ops, SparseCore 0:
  74.8 85.1 all-gather.1
  185.3 172.7 all-reduce.1
